TPU v7x, 1024 devices: a whole 8x8x8 slice. The times are simulated.
1024 devices in a mesh: seq: 64 (over z, y), head: 16 (over x, core).
Axes of the slice: x: 8, y: 8, z: 8, core: 2. Of those that a mesh axis runs over, the one named last changes fastest.
Arguments:
- queries: bfloat16 [32768, 4096], P(('seq', 'head')), may hold values from -100 to 100
- keys_in: bfloat16 [32768, 4096], P(('seq', 'head')), may hold values from -16 to 16
- values_in: bfloat16 [32768, 4096], P(('seq', 'head')), may hold values from -16 to 16
- grad_out: bfloat16 [32768, 4096], P(('seq', 'head')), may hold values from -6 to 6
Outputs:
- attended: bfloat16 [32768, 4096], P(('seq', 'head'))
- grad_queries: bfloat16 [32768, 4096], P(('seq', 'head'))
- grad_keys: bfloat16 [32768, 4096], P(('seq', 'head'))
- grad_values: bfloat16 [32768, 4096], P(('seq', 'head'))
All inputs are finite; a program needn't handle non-finite values.
Results may differ from a plain program's by a relative error of at most 0.0052.
Values may be sent and summed in bfloat16 or wider, within the bound.
A program may use at most 32 MiB of HBM per device.

v0:
```python
import jax
import jax.numpy as jnp
from jax import lax
from jax.sharding import PartitionSpec as P

HD = 128
CROWS = 16


def swapped(block, axis, apart):
    count = lax.axis_size(axis)
    route = []
    for low in range(count):
        high = low | 1 << apart
        if high != low and high < count:
            route += [(low, high), (high, low)]
    return lax.ppermute(block, axis, route)


def on_device(queries, keys_in, values_in, grad_out):
    seq_count = lax.axis_size("seq")
    depth = seq_count.bit_length() - 1
    scale_q = HD ** (-0.5)
    query_here, key_here, value_here, grad_here = (
        lax.all_to_all(queries, "head", split_axis=1, concat_axis=0, tiled=True),
        lax.all_to_all(keys_in, "head", split_axis=1, concat_axis=0, tiled=True),
        lax.all_to_all(values_in, "head", split_axis=1, concat_axis=0, tiled=True),
        lax.all_to_all(grad_out, "head", split_axis=1, concat_axis=0, tiled=True),
    )
    rows_here = query_here.shape[0]
    head_count = query_here.shape[1] // HD
    pool_size = rows_here // CROWS
    query_three = query_here.reshape(rows_here, head_count, HD)
    key_three = key_here.reshape(rows_here, head_count, HD)
    value_three = value_here.reshape(rows_here, head_count, HD)
    grad_three = grad_here.reshape(rows_here, head_count, HD)
    pooled_k = jnp.mean(
        key_three.astype(jnp.float32).reshape(CROWS, pool_size, head_count, HD), axis=1
    ).transpose(1, 0, 2)
    pooled_v = jnp.mean(
        value_three.astype(jnp.float32).reshape(CROWS, pool_size, head_count, HD), axis=1
    ).transpose(1, 0, 2)
    own_pooled = jnp.stack([pooled_k, pooled_v], axis=0)
    siblings = []
    mean_now = own_pooled
    for level in range(depth):
        received = swapped(mean_now, "seq", level)
        siblings.append(received)
        mean_now = 0.5 * (mean_now + received)
    coarse = (
        jnp.stack(siblings, axis=2).reshape(2, head_count, depth * CROWS, HD).astype(jnp.bfloat16)
    )
    log_counts = jnp.repeat(
        jnp.log(float(pool_size) * 2.0 ** jnp.arange(depth, dtype=jnp.float32)), CROWS
    )
    offsets = jnp.concatenate([jnp.zeros((rows_here,), jnp.float32), log_counts])
    keys_full = jnp.concatenate([key_three.transpose(1, 0, 2), coarse[0]], axis=1)
    values_full = jnp.concatenate([value_three.transpose(1, 0, 2), coarse[1]], axis=1)
    scores = (
        jnp.einsum("shd,htd->hst", query_three, keys_full, preferred_element_type=jnp.float32)
        * scale_q
        + offsets
    )
    probs = jax.nn.softmax(scores, axis=-1)
    probs_low = probs.astype(jnp.bfloat16)
    attended = jnp.einsum(
        "hst,htd->shd", probs_low, values_full, preferred_element_type=jnp.float32
    ).astype(jnp.bfloat16)
    dprob = jnp.einsum("shd,htd->hst", grad_three, values_full, preferred_element_type=jnp.float32)
    dscore = (scale_q * probs * (dprob - jnp.sum(probs * dprob, axis=-1, keepdims=True))).astype(
        jnp.bfloat16
    )
    grad_query = jnp.einsum(
        "hst,htd->shd", dscore, keys_full, preferred_element_type=jnp.float32
    ).astype(jnp.bfloat16)
    dkeys = jnp.einsum("hst,shd->htd", dscore, query_three, preferred_element_type=jnp.float32)
    dvalues = jnp.einsum("hst,shd->htd", probs_low, grad_three, preferred_element_type=jnp.float32)
    coarse_grad = jnp.stack([dkeys[:, rows_here:], dvalues[:, rows_here:]], axis=0).reshape(
        2, head_count, depth, CROWS, HD
    )
    grad_above = jnp.zeros((2, head_count, CROWS, HD), jnp.float32)
    for level in reversed(range(depth)):
        outgoing = coarse_grad[:, :, level] + 0.5 * grad_above
        grad_above = 0.5 * grad_above + swapped(outgoing, "seq", level)
    spread = jnp.broadcast_to(
        (grad_above / float(pool_size))[:, :, :, None, :], (2, head_count, CROWS, pool_size, HD)
    )
    spread = spread.reshape(2, head_count, rows_here, HD)
    grad_key = (dkeys[:, :rows_here] + spread[0]).transpose(1, 0, 2).astype(jnp.bfloat16)
    grad_value = (dvalues[:, :rows_here] + spread[1]).transpose(1, 0, 2).astype(jnp.bfloat16)
    width_here = head_count * HD
    return (
        lax.all_to_all(
            attended.reshape(rows_here, width_here), "head", split_axis=0, concat_axis=1, tiled=True
        ),
        lax.all_to_all(
            grad_query.reshape(rows_here, width_here),
            "head",
            split_axis=0,
            concat_axis=1,
            tiled=True,
        ),
        lax.all_to_all(
            grad_key.reshape(rows_here, width_here), "head", split_axis=0, concat_axis=1, tiled=True
        ),
        lax.all_to_all(
            grad_value.reshape(rows_here, width_here),
            "head",
            split_axis=0,
            concat_axis=1,
            tiled=True,
        ),
    )


def solution(mesh):
    placed = (
        P(("seq", "head"), None),
        P(("seq", "head"), None),
        P(("seq", "head"), None),
        P(("seq", "head"), None),
    )
    return jax.shard_map(
        on_device,
        mesh=mesh,
        in_specs=placed,
        out_specs=(
            P(("seq", "head"), None),
            P(("seq", "head"), None),
            P(("seq", "head"), None),
            P(("seq", "head"), None),
        ),
        check_vma=False,
    )
```

profile of v0, /device:TPU:1, one launch (start us, length us, event | category | flops | bytes accessed | tf_op | source)
XLA Modules:
  0.0 215.4 jit_solution(8306054997219746828)
XLA Ops:
  2.4 17.5 %all-to-all-start = ((bf16[32,16,256]{2,0,1:T(8,128)(2,1)}), bf16[32,16,256]{2,0,1:T(8,128)(2,1)S(1)}, u32[]{:S(2)}, u32[]{:S(2)}) async-start(bf16[32,16,256]{2,0,1:T(8,128)(2,1)} %bitcast.117), calls=%async_computation | async-start | bytes 524288 | tf_op jit(solution)/shard_map/all_to_all | solution.py:27
  21.5 10.2 %all-to-all-done = bf16[32,16,256]{2,0,1:T(8,128)(2,1)S(1)} async-done(((bf16[32,16,256]{2,0,1:T(8,128)(2,1)}), bf16[32,16,256]{2,0,1:T(8,128)(2,1)S(1)}, u32[]{:S(2)}, u32[]{:S(2)}) %all-to-all-start) | async-done | bytes 262176 | tf_op jit(solution)/shard_map/all_to_all | solution.py:27
  31.7 3.4 %all-to-all-start.1 = ((bf16[32,16,256]{2,0,1:T(8,128)(2,1)}), bf16[32,16,256]{2,0,1:T(8,128)(2,1)S(1)}, u32[]{:S(2)}, u32[]{:S(2)}) async-start(bf16[32,16,256]{2,0,1:T(8,128)(2,1)} %bitcast.116), calls=%async_computation.1 | async-start | bytes 524288 | tf_op jit(solution)/shard_map/all_to_all | solution.py:26
  36.8 9.3 %all-to-all-done.1 = bf16[32,16,256]{2,0,1:T(8,128)(2,1)S(1)} async-done(((bf16[32,16,256]{2,0,1:T(8,128)(2,1)}), bf16[32,16,256]{2,0,1:T(8,128)(2,1)S(1)}, u32[]{:S(2)}, u32[]{:S(2)}) %all-to-all-start.1) | async-done | bytes 262176 | tf_op jit(solution)/shard_map/all_to_all | solution.py:26
  46.1 3.4 %all-to-all-start.2 = ((bf16[32,16,256]{2,0,1:T(8,128)(2,1)}), bf16[32,16,256]{2,0,1:T(8,128)(2,1)S(1)}, u32[]{:S(2)}, u32[]{:S(2)}) async-start(bf16[32,16,256]{2,0,1:T(8,128)(2,1)} %bitcast.115), calls=%async_computation.2 | async-start | bytes 524288 | tf_op jit(solution)/shard_map/all_to_all | solution.py:25
  50.4 10.6 %all-to-all-done.2 = bf16[32,16,256]{2,0,1:T(8,128)(2,1)S(1)} async-done(((bf16[32,16,256]{2,0,1:T(8,128)(2,1)}), bf16[32,16,256]{2,0,1:T(8,128)(2,1)S(1)}, u32[]{:S(2)}, u32[]{:S(2)}) %all-to-all-start.2) | async-done | bytes 262176 | tf_op jit(solution)/shard_map/all_to_all | solution.py:25
  61.0 3.4 %all-to-all-start.4 = ((bf16[32,16,256]{2,0,1:T(8,128)(2,1)}), bf16[32,16,256]{2,0,1:T(8,128)(2,1)S(1)}, u32[]{:S(2)}, u32[]{:S(2)}) async-start(bf16[32,16,256]{2,0,1:T(8,128)(2,1)} %bitcast.114), calls=%async_computation.4 | async-start | bytes 524288 | tf_op jit(solution)/shard_map/all_to_all | solution.py:28
  67.0 9.1 %all-to-all-done.4 = bf16[32,16,256]{2,0,1:T(8,128)(2,1)S(1)} async-done(((bf16[32,16,256]{2,0,1:T(8,128)(2,1)}), bf16[32,16,256]{2,0,1:T(8,128)(2,1)S(1)}, u32[]{:S(2)}, u32[]{:S(2)}) %all-to-all-start.4) | async-done | bytes 262176 | tf_op jit(solution)/shard_map/all_to_all | solution.py:28
  78.2 4.2 %collective-permute-done.1 = f32[2,2,16,128]{3,1,2,0:T(2,128)S(1)} collective-permute-done((f32[2,2,16,128]{3,1,2,0:T(2,128)S(1)}, f32[2,2,16,128]{3,1,2,0:T(2,128)S(1)}, u32[]{:S(2)}, u32[]{:S(2)}) %collective-permute-start.1) | collective-permute-done | bytes 32800 | tf_op jit(solution)/shard_map/ppermute | solution.py:17
  84.4 6.6 %collective-permute-done.2 = f32[2,2,16,128]{3,1,2,0:T(2,128)S(1)} collective-permute-done((f32[2,2,16,128]{3,1,2,0:T(2,128)S(1)}, f32[2,2,16,128]{3,1,2,0:T(2,128)S(1)}, u32[]{:S(2)}, u32[]{:S(2)}) %collective-permute-start.2) | collective-permute-done | bytes 32800 | tf_op jit(solution)/shard_map/ppermute | solution.py:17
  97.7 3.7 %collective-permute-done.4 = f32[2,2,16,128]{3,1,2,0:T(2,128)S(1)} collective-permute-done((f32[2,2,16,128]{3,1,2,0:T(2,128)S(1)}, f32[2,2,16,128]{3,1,2,0:T(2,128)S(1)}, u32[]{:S(2)}, u32[]{:S(2)}) %collective-permute-start.4) | collective-permute-done | bytes 32800 | tf_op jit(solution)/shard_map/ppermute | solution.py:17
  101.4 7.9 %collective-permute-start.5 = (bf16[2,2,16,128]{3,1,2,0:T(2,128)(2,1)S(1)}, bf16[2,2,16,128]{3,1,2,0:T(2,128)(2,1)S(1)}, u32[]{:S(2)}, u32[]{:S(2)}) collective-permute-start(bf16[2,2,16,128]{3,1,2,0:T(2,128)(2,1)S(1)} %add_multiply_fusion.5), channel_id=1, source_target_pairs={{0,512},{512,0},{16,528},{528,16},{32,544},{544,32},{48,560},{560,... | collective-permute-start | bytes 49160 | tf_op jit(solution)/shard_map/ppermute | solution.py:17
  118.6 7.4 %collective-permute-start.6 = (f32[2,2,16,128]{3,1,2,0:T(2,128)S(1)}, f32[2,2,16,128]{3,1,2,0:T(2,128)S(1)}, u32[]{:S(2)}, u32[]{:S(2)}) collective-permute-start(f32[2,2,16,128]{3,1,2,0:T(2,128)S(1)} %slice_bitcast_fusion.5), channel_id=1, source_target_pairs={{0,512},{512,0},{16,528},{528,16},{32,544},{544,32},{48,560},{560,... | collective-permute-start | bytes 98312 | tf_op jit(solution)/shard_map/ppermute | solution.py:17
  127.3 4.6 %collective-permute-start.7 = (f32[2,2,16,128]{3,1,2,0:T(2,128)S(1)}, f32[2,2,16,128]{3,1,2,0:T(2,128)S(1)}, u32[]{:S(2)}, u32[]{:S(2)}) collective-permute-start(f32[2,2,16,128]{3,1,2,0:T(2,128)S(1)} %fusion.35), channel_id=1, source_target_pairs={{0,256},{256,0},{16,272},{272,16},{32,288},{288,32},{48,304},{304,... | collective-permute-start | bytes 98312 | tf_op jit(solution)/shard_map/ppermute | solution.py:17
  138.3 7.7 %collective-permute-start.9 = (f32[2,2,16,128]{3,1,2,0:T(2,128)S(1)}, f32[2,2,16,128]{3,1,2,0:T(2,128)S(1)}, u32[]{:S(2)}, u32[]{:S(2)}) collective-permute-start(f32[2,2,16,128]{3,1,2,0:T(2,128)S(1)} %fusion.33), channel_id=1, source_target_pairs={{0,64},{64,0},{16,80},{80,16},{32,96},{96,32},{48,112},{112,48},{1... | collective-permute-start | bytes 98312 | tf_op jit(solution)/shard_map/ppermute | solution.py:17
  147.6 10.9 %all-to-all-start.3 = ((bf16[16,32,256]{2,1,0:T(8,128)(2,1)}), bf16[16,32,256]{2,1,0:T(8,128)(2,1)S(1)}, u32[]{:S(2)}, u32[]{:S(2)}) async-start(bf16[16,32,256]{2,1,0:T(8,128)(2,1)} %all_to_all.113), calls=%async_computation.3 | async-start | bytes 524288 | tf_op jit(solution)/shard_map/all_to_all | solution.py:93
  161.9 8.4 %all-to-all-done.3 = bf16[16,32,256]{2,1,0:T(8,128)(2,1)S(1)} async-done(((bf16[16,32,256]{2,1,0:T(8,128)(2,1)}), bf16[16,32,256]{2,1,0:T(8,128)(2,1)S(1)}, u32[]{:S(2)}, u32[]{:S(2)}) %all-to-all-start.3) | async-done | bytes 262176 | tf_op jit(solution)/shard_map/all_to_all | solution.py:93
  170.3 3.4 %all-to-all-start.5 = ((bf16[16,32,256]{2,1,0:T(8,128)(2,1)}), bf16[16,32,256]{2,1,0:T(8,128)(2,1)S(1)}, u32[]{:S(2)}, u32[]{:S(2)}) async-start(bf16[16,32,256]{2,1,0:T(8,128)(2,1)} %all_to_all.120), calls=%async_computation.5 | async-start | bytes 524288 | tf_op jit(solution)/shard_map/all_to_all | solution.py:96
  175.7 3.3 %collective-permute-done.11 = f32[2,2,16,128]{3,1,2,0:T(2,128)S(1)} collective-permute-done((f32[2,2,16,128]{3,1,2,0:T(2,128)S(1)}, f32[2,2,16,128]{3,1,2,0:T(2,128)S(1)}, u32[]{:S(2)}, u32[]{:S(2)}) %collective-permute-start.11) | collective-permute-done | bytes 32800 | tf_op jit(solution)/shard_map/ppermute | solution.py:17
  180.3 4.5 %all-to-all-done.5 = bf16[16,32,256]{2,1,0:T(8,128)(2,1)S(1)} async-done(((bf16[16,32,256]{2,1,0:T(8,128)(2,1)}), bf16[16,32,256]{2,1,0:T(8,128)(2,1)S(1)}, u32[]{:S(2)}, u32[]{:S(2)}) %all-to-all-start.5) | async-done | bytes 262176 | tf_op jit(solution)/shard_map/all_to_all | solution.py:96
  184.7 3.4 %all-to-all-start.6 = ((bf16[16,32,256]{2,1,0:T(8,128)(2,1)}), bf16[16,32,256]{2,1,0:T(8,128)(2,1)S(1)}, u32[]{:S(2)}, u32[]{:S(2)}) async-start(bf16[16,32,256]{2,1,0:T(8,128)(2,1)} %all_to_all.124), calls=%async_computation.6 | async-start | bytes 524288 | tf_op jit(solution)/shard_map/all_to_all | solution.py:103
  189.4 10.2 %all-to-all-done.6 = bf16[16,32,256]{2,1,0:T(8,128)(2,1)S(1)} async-done(((bf16[16,32,256]{2,1,0:T(8,128)(2,1)}), bf16[16,32,256]{2,1,0:T(8,128)(2,1)S(1)}, u32[]{:S(2)}, u32[]{:S(2)}) %all-to-all-start.6) | async-done | bytes 262176 | tf_op jit(solution)/shard_map/all_to_all | solution.py:103
  199.6 3.4 %all-to-all-start.7 = ((bf16[16,32,256]{2,1,0:T(8,128)(2,1)}), bf16[16,32,256]{2,1,0:T(8,128)(2,1)S(1)}, u32[]{:S(2)}, u32[]{:S(2)}) async-start(bf16[16,32,256]{2,1,0:T(8,128)(2,1)} %all_to_all.128), calls=%async_computation.7 | async-start | bytes 524288 | tf_op jit(solution)/shard_map/all_to_all | solution.py:106
  205.2 9.5 %all-to-all-done.7 = bf16[16,32,256]{2,1,0:T(8,128)(2,1)S(1)} async-done(((bf16[16,32,256]{2,1,0:T(8,128)(2,1)}), bf16[16,32,256]{2,1,0:T(8,128)(2,1)S(1)}, u32[]{:S(2)}, u32[]{:S(2)}) %all-to-all-start.7) | async-done | bytes 262176 | tf_op jit(solution)/shard_map/all_to_all | solution.py:106
  (100 shorter events, 48.0 us)
Async XLA Ops:
  0.6 49.0 %copy-start.4 = (bf16[32,4096]{1,0:T(8,128)(2,1)S(1)}, bf16[32,4096]{1,0:T(8,128)(2,1)}, u32[]{:S(2)}) copy-start(bf16[32,4096]{1,0:T(8,128)(2,1)} %param.7) | copy-start | bytes 786436
  2.4 29.3 %all-to-all-start = ((bf16[32,16,256]{2,0,1:T(8,128)(2,1)}), bf16[32,16,256]{2,0,1:T(8,128)(2,1)S(1)}, u32[]{:S(2)}, u32[]{:S(2)}) async-start(bf16[32,16,256]{2,0,1:T(8,128)(2,1)} %bitcast.117), calls=%async_computation | async-start | bytes 524288 | tf_op jit(solution)/shard_map/all_to_all | solution.py:27
  31.7 14.5 %all-to-all-start.1 = ((bf16[32,16,256]{2,0,1:T(8,128)(2,1)}), bf16[32,16,256]{2,0,1:T(8,128)(2,1)S(1)}, u32[]{:S(2)}, u32[]{:S(2)}) async-start(bf16[32,16,256]{2,0,1:T(8,128)(2,1)} %bitcast.116), calls=%async_computation.1 | async-start | bytes 524288 | tf_op jit(solution)/shard_map/all_to_all | solution.py:26
  46.1 14.9 %all-to-all-start.2 = ((bf16[32,16,256]{2,0,1:T(8,128)(2,1)}), bf16[32,16,256]{2,0,1:T(8,128)(2,1)S(1)}, u32[]{:S(2)}, u32[]{:S(2)}) async-start(bf16[32,16,256]{2,0,1:T(8,128)(2,1)} %bitcast.115), calls=%async_computation.2 | async-start | bytes 524288 | tf_op jit(solution)/shard_map/all_to_all | solution.py:25
  61.0 15.1 %all-to-all-start.4 = ((bf16[32,16,256]{2,0,1:T(8,128)(2,1)}), bf16[32,16,256]{2,0,1:T(8,128)(2,1)S(1)}, u32[]{:S(2)}, u32[]{:S(2)}) async-start(bf16[32,16,256]{2,0,1:T(8,128)(2,1)} %bitcast.114), calls=%async_computation.4 | async-start | bytes 524288 | tf_op jit(solution)/shard_map/all_to_all | solution.py:28
  64.6 11.6 %collective-permute-start = (f32[2,2,16,128]{3,1,2,0:T(2,128)S(1)}, f32[2,2,16,128]{3,1,2,0:T(2,128)S(1)}, u32[]{:S(2)}, u32[]{:S(2)}) collective-permute-start(f32[2,2,16,128]{3,1,2,0:T(2,128)S(1)} %pad_maximum_fusion.9), channel_id=1, source_target_pairs={{0,16},{16,0},{32,48},{48,32},{64,80},{80,64},{96,112},{112,96},{1... | collective-permute-start | bytes 98312 | tf_op jit(solution)/shard_map/ppermute | solution.py:17
  76.2 6.2 %collective-permute-start.1 = (f32[2,2,16,128]{3,1,2,0:T(2,128)S(1)}, f32[2,2,16,128]{3,1,2,0:T(2,128)S(1)}, u32[]{:S(2)}, u32[]{:S(2)}) collective-permute-start(f32[2,2,16,128]{3,1,2,0:T(2,128)S(1)} %add_multiply_fusion.9), channel_id=1, source_target_pairs={{0,32},{32,0},{16,48},{48,16},{64,96},{96,64},{80,112},{112,80},{1... | collective-permute-start | bytes 98312 | tf_op jit(solution)/shard_map/ppermute | solution.py:17
  82.4 8.6 %collective-permute-start.2 = (f32[2,2,16,128]{3,1,2,0:T(2,128)S(1)}, f32[2,2,16,128]{3,1,2,0:T(2,128)S(1)}, u32[]{:S(2)}, u32[]{:S(2)}) collective-permute-start(f32[2,2,16,128]{3,1,2,0:T(2,128)S(1)} %add_multiply_fusion.8), channel_id=1, source_target_pairs={{0,64},{64,0},{16,80},{80,16},{32,96},{96,32},{48,112},{112,48},{1... | collective-permute-start | bytes 98312 | tf_op jit(solution)/shard_map/ppermute | solution.py:17
  91.0 4.7 %collective-permute-start.3 = (f32[2,2,16,128]{3,1,2,0:T(2,128)S(1)}, f32[2,2,16,128]{3,1,2,0:T(2,128)S(1)}, u32[]{:S(2)}, u32[]{:S(2)}) collective-permute-start(f32[2,2,16,128]{3,1,2,0:T(2,128)S(1)} %add_multiply_fusion.7), channel_id=1, source_target_pairs={{0,128},{128,0},{16,144},{144,16},{32,160},{160,32},{48,176},{176,... | collective-permute-start | bytes 98312 | tf_op jit(solution)/shard_map/ppermute | solution.py:17
  95.7 5.6 %collective-permute-start.4 = (f32[2,2,16,128]{3,1,2,0:T(2,128)S(1)}, f32[2,2,16,128]{3,1,2,0:T(2,128)S(1)}, u32[]{:S(2)}, u32[]{:S(2)}) collective-permute-start(f32[2,2,16,128]{3,1,2,0:T(2,128)S(1)} %add_multiply_fusion.6), channel_id=1, source_target_pairs={{0,256},{256,0},{16,272},{272,16},{32,288},{288,32},{48,304},{304,... | collective-permute-start | bytes 98312 | tf_op jit(solution)/shard_map/ppermute | solution.py:17
  101.4 9.1 %collective-permute-start.5 = (bf16[2,2,16,128]{3,1,2,0:T(2,128)(2,1)S(1)}, bf16[2,2,16,128]{3,1,2,0:T(2,128)(2,1)S(1)}, u32[]{:S(2)}, u32[]{:S(2)}) collective-permute-start(bf16[2,2,16,128]{3,1,2,0:T(2,128)(2,1)S(1)} %add_multiply_fusion.5), channel_id=1, source_target_pairs={{0,512},{512,0},{16,528},{528,16},{32,544},{544,32},{48,560},{560,... | collective-permute-start | bytes 49160 | tf_op jit(solution)/shard_map/ppermute | solution.py:17
  117.9 28.2 %copy-start.1 = (f32[2,512,608]{1,2,0:T(8,128)S(1)}, f32[2,512,608]{1,2,0:T(8,128)}, u32[]{:S(2)}) copy-start(f32[2,512,608]{1,2,0:T(8,128)} %copy-done) | copy-start | bytes 7471108
  118.6 8.7 %collective-permute-start.6 = (f32[2,2,16,128]{3,1,2,0:T(2,128)S(1)}, f32[2,2,16,128]{3,1,2,0:T(2,128)S(1)}, u32[]{:S(2)}, u32[]{:S(2)}) collective-permute-start(f32[2,2,16,128]{3,1,2,0:T(2,128)S(1)} %slice_bitcast_fusion.5), channel_id=1, source_target_pairs={{0,512},{512,0},{16,528},{528,16},{32,544},{544,32},{48,560},{560,... | collective-permute-start | bytes 98312 | tf_op jit(solution)/shard_map/ppermute | solution.py:17
  127.3 6.3 %collective-permute-start.7 = (f32[2,2,16,128]{3,1,2,0:T(2,128)S(1)}, f32[2,2,16,128]{3,1,2,0:T(2,128)S(1)}, u32[]{:S(2)}, u32[]{:S(2)}) collective-permute-start(f32[2,2,16,128]{3,1,2,0:T(2,128)S(1)} %fusion.35), channel_id=1, source_target_pairs={{0,256},{256,0},{16,272},{272,16},{32,288},{288,32},{48,304},{304,... | collective-permute-start | bytes 98312 | tf_op jit(solution)/shard_map/ppermute | solution.py:17
  133.6 4.7 %collective-permute-start.8 = (f32[2,2,16,128]{3,1,2,0:T(2,128)S(1)}, f32[2,2,16,128]{3,1,2,0:T(2,128)S(1)}, u32[]{:S(2)}, u32[]{:S(2)}) collective-permute-start(f32[2,2,16,128]{3,1,2,0:T(2,128)S(1)} %fusion.34), channel_id=1, source_target_pairs={{0,128},{128,0},{16,144},{144,16},{32,160},{160,32},{48,176},{176,... | collective-permute-start | bytes 98312 | tf_op jit(solution)/shard_map/ppermute | solution.py:17
  138.3 22.1 %copy-start.5 = (bf16[1,2,6,16,128]{4,3,2,1,0:T(8,128)(2,1)S(1)}, bf16[1,2,6,16,128]{4,3,2,1,0:T(8,128)(2,1)}, u32[]{:S(2)}) copy-start(bf16[1,2,6,16,128]{4,3,2,1,0:T(8,128)(2,1)} %copy.42) | copy-start | bytes 147460
  138.3 20.1 %collective-permute-start.9 = (f32[2,2,16,128]{3,1,2,0:T(2,128)S(1)}, f32[2,2,16,128]{3,1,2,0:T(2,128)S(1)}, u32[]{:S(2)}, u32[]{:S(2)}) collective-permute-start(f32[2,2,16,128]{3,1,2,0:T(2,128)S(1)} %fusion.33), channel_id=1, source_target_pairs={{0,64},{64,0},{16,80},{80,16},{32,96},{96,32},{48,112},{112,48},{1... | collective-permute-start | bytes 98312 | tf_op jit(solution)/shard_map/ppermute | solution.py:17
  147.6 22.7 %all-to-all-start.3 = ((bf16[16,32,256]{2,1,0:T(8,128)(2,1)}), bf16[16,32,256]{2,1,0:T(8,128)(2,1)S(1)}, u32[]{:S(2)}, u32[]{:S(2)}) async-start(bf16[16,32,256]{2,1,0:T(8,128)(2,1)} %all_to_all.113), calls=%async_computation.3 | async-start | bytes 524288 | tf_op jit(solution)/shard_map/all_to_all | solution.py:93
  158.5 15.2 %collective-permute-start.10 = (f32[2,2,16,128]{3,1,2,0:T(2,128)S(1)}, f32[2,2,16,128]{3,1,2,0:T(2,128)S(1)}, u32[]{:S(2)}, u32[]{:S(2)}) collective-permute-start(f32[2,2,16,128]{3,1,2,0:T(2,128)S(1)} %get-tuple-element.4), channel_id=1, source_target_pairs={{0,32},{32,0},{16,48},{48,16},{64,96},{96,64},{80,112},{112,80},{1... | collective-permute-start | bytes 98312 | tf_op jit(solution)/shard_map/ppermute | solution.py:17
  160.9 27.3 %copy-start.3 = (f32[2,608,128]{2,1,0:T(8,128)S(1)}, f32[2,608,128]{2,1,0:T(8,128)}, u32[]{:S(2)}) copy-start(f32[2,608,128]{2,1,0:T(8,128)} %copy-done.2) | copy-start | bytes 1867780
  170.3 14.5 %all-to-all-start.5 = ((bf16[16,32,256]{2,1,0:T(8,128)(2,1)}), bf16[16,32,256]{2,1,0:T(8,128)(2,1)S(1)}, u32[]{:S(2)}, u32[]{:S(2)}) async-start(bf16[16,32,256]{2,1,0:T(8,128)(2,1)} %all_to_all.120), calls=%async_computation.5 | async-start | bytes 524288 | tf_op jit(solution)/shard_map/all_to_all | solution.py:96
  173.8 5.2 %collective-permute-start.11 = (f32[2,2,16,128]{3,1,2,0:T(2,128)S(1)}, f32[2,2,16,128]{3,1,2,0:T(2,128)S(1)}, u32[]{:S(2)}, u32[]{:S(2)}) collective-permute-start(f32[2,2,16,128]{3,1,2,0:T(2,128)S(1)} %fusion.31), channel_id=1, source_target_pairs={{0,16},{16,0},{32,48},{48,32},{64,80},{80,64},{96,112},{112,96},{1... | collective-permute-start | bytes 98312 | tf_op jit(solution)/shard_map/ppermute | solution.py:17
  184.7 14.9 %all-to-all-start.6 = ((bf16[16,32,256]{2,1,0:T(8,128)(2,1)}), bf16[16,32,256]{2,1,0:T(8,128)(2,1)S(1)}, u32[]{:S(2)}, u32[]{:S(2)}) async-start(bf16[16,32,256]{2,1,0:T(8,128)(2,1)} %all_to_all.124), calls=%async_computation.6 | async-start | bytes 524288 | tf_op jit(solution)/shard_map/all_to_all | solution.py:103
  199.6 15.1 %all-to-all-start.7 = ((bf16[16,32,256]{2,1,0:T(8,128)(2,1)}), bf16[16,32,256]{2,1,0:T(8,128)(2,1)S(1)}, u32[]{:S(2)}, u32[]{:S(2)}) async-start(bf16[16,32,256]{2,1,0:T(8,128)(2,1)} %all_to_all.128), calls=%async_computation.7 | async-start | bytes 524288 | tf_op jit(solution)/shard_map/all_to_all | solution.py:106
  (3 other events, 7.3 us)
where the time goes:
time: 217 us; the launch traced here: 215 us
  waiting for transfers between devices  98.3 us (45%)
  starting transfers between devices  92.7 us (43%)
  local copies, waits for them, and re-layouts  16.1 us (7%)
  matrix products  4.03 us (2%)
  other arithmetic  3.07 us (1%)
    ppermute x12, starting transfers between devices, swapped(): return lax.ppermute(block, axis, route)  43.8 us
    ppermute x12, waiting for transfers between devices, swapped(): return lax.ppermute(block, axis, route)  26.5 us
    all_to_all x1, starting transfers between devices, on_device(): lax.all_to_all(values_in, 'head', split_axis=1, concat_axis=0, tiled=True)  17.5 us
    all_to_all x1, starting transfers between devices, on_device(): lax.all_to_all(attended.reshape(rows_here, width_here), 'head', split_axi...  10.9 us
    all_to_all x1, waiting for transfers between devices, on_device(): lax.all_to_all(queries, 'head', split_axis=1, concat_axis=0, tiled=True)  10.6 us
    all_to_all x1, waiting for transfers between devices, on_device(): lax.all_to_all(grad_key.reshape(rows_here, width_here), 'head', split_axi...  10.2 us
    all_to_all x1, waiting for transfers between devices, on_device(): lax.all_to_all(values_in, 'head', split_axis=1, concat_axis=0, tiled=True)  10.2 us
    all_to_all x1, waiting for transfers between devices, on_device(): lax.all_to_all(grad_value.reshape(rows_here, width_here), 'head', split_a...  9.49 us
  transfers between devices with their start and end apart: 20, of which 17 were waited for; matrix products, arithmetic and copies ran while one was open for 4% of the time, Pallas kernels for 0%

commit v1 on v0

v1 whole, which is shorter than its diff:
```python
import functools
import math

import jax
import jax.numpy as jnp
from jax import lax
from jax.experimental import pallas as pl
from jax.experimental.pallas import tpu as pltpu
from jax.sharding import PartitionSpec as P

HD = 128
MESH = pl.DeviceIdType.MESH
F32 = jnp.float32
BF16 = jnp.bfloat16

S_POOL, S_K, S_V, S_Q, S_G, S_YF, S_ZF, S_ZB, S_YB, S_OUT = 0, 1, 2, 3, 5, 7, 9, 11, 13, 15
N_SEMS = 19


def flip(index, mask):
    out = index
    bit = 1
    while bit <= mask:
        if mask & bit:
            out = out + bit * (1 - 2 * ((index // bit) % 2))
        bit *= 2
    return out


def kernel(sizes, *refs):
    nx, ny, nz = sizes
    (q_in, k_in, v_in, g_in, o_out, dq_out, dk_out, dv_out,
     kl, vl, ps, pr, qr, kr, vr, gr, yr, zr, kc, vc, zs, zb, ys, yb,
     os, dqs, dks, dvs, dka, dva, dkc, dvc, local_sem, send, recv) = refs
    ins = (q_in, k_in, v_in, g_in)
    outs = (o_out, dq_out, dk_out, dv_out)
    nh = nx * 2
    rows = q_in.shape[0]
    shard = nh * rows
    ly, lz = ny.bit_length() - 1, nz.bit_length() - 1
    levels = ly + lz
    crows = nh
    scale = HD ** (-0.5)

    s_me = lax.axis_index("seq")
    h_me = lax.axis_index("head")
    y_me, z_me = s_me % ny, s_me // ny
    x_me, c_me = h_me // 2, h_me % 2

    def ahead(slot):
        k, f = slot // 2, slot % 2
        return ((x_me + k) % nx) * 2 + (c_me if f == 0 else 1 - c_me)

    def behind(slot):
        k, f = slot // 2, slot % 2
        return ((x_me + nx - k) % nx) * 2 + (c_me if f == 0 else 1 - c_me)

    order = []
    for k in range(nx // 2, -1, -1):
        for kk in dict.fromkeys((k, (nx - k) % nx)):
            order += [2 * kk, 2 * kk + 1]
    order = [s for s in order if s != 0]

    def y_dev(k):
        return (z_me * ny + flip(y_me, k), h_me)

    def z_dev(k):
        return (flip(z_me, k) * ny + y_me, h_me)

    kcopy = pltpu.make_async_copy(k_in, kl, local_sem.at[0])
    vcopy = pltpu.make_async_copy(v_in, vl, local_sem.at[1])
    kcopy.start()
    vcopy.start()
    barrier = pltpu.get_barrier_semaphore()
    for s in order:
        pl.semaphore_signal(barrier, inc=1, device_id=(s_me, ahead(s)), device_id_type=MESH)
    for k in range(1, ny):
        pl.semaphore_signal(barrier, inc=1, device_id=y_dev(k), device_id_type=MESH)
    for k in range(1, nz):
        pl.semaphore_signal(barrier, inc=1, device_id=z_dev(k), device_id_type=MESH)

    kcopy.wait()
    vcopy.wait()
    for d in range(nh):
        for h in range(2):
            cols = pl.ds((d * 2 + h) * HD, HD)
            for kv, ref in enumerate((kl, vl)):
                mean = jnp.sum(ref[:, cols].astype(F32), axis=0, keepdims=True) * (1.0 / rows)
                ps[d, pl.ds(h * 2 + kv, 1), :] = mean

    pl.semaphore_wait(barrier, len(order) + ny - 1 + nz - 1)

    def remote(src, dst, sem, device):
        pltpu.make_async_remote_copy(
            src_ref=src, dst_ref=dst, send_sem=send.at[sem], recv_sem=recv.at[sem],
            device_id=device, device_id_type=MESH,
        ).start()

    def drain(ref, sem):
        pltpu.make_async_copy(ref, ref, sem).wait()

    for s in order:
        d = ahead(s)
        remote(ps.at[d], pr.at[s], S_POOL, (s_me, d))
    pr[0] = ps[h_me]

    def scatter_in(src, dst, sem, first, width):
        def piece(d):
            start = pl.multiple_of(d * 2 * HD + first, HD)
            return src.at[:, pl.ds(start, width)]

        for s in order:
            d = ahead(s)
            remote(piece(d), dst.at[pl.ds(s * rows, rows), pl.ds(first, width)], sem, (s_me, d))
        pltpu.make_async_copy(
            piece(h_me), dst.at[pl.ds(0, rows), pl.ds(first, width)], recv.at[sem]
        ).start()

    scatter_in(k_in, kr, S_K, 0, 2 * HD)
    scatter_in(v_in, vr, S_V, 0, 2 * HD)
    for h in range(2):
        scatter_in(q_in, qr, S_Q + h, h * HD, HD)
        scatter_in(g_in, gr, S_G + h, h * HD, HD)

    drain(pr.at[pl.ds(1, nh - 1)], recv.at[S_POOL])
    for h in range(2):
        for kv in range(2):
            yr[h, 0, pl.ds(kv * crows, crows), :] = pr[:, h * 2 + kv, :]
        for k in range(1, ny):
            remote(yr.at[h, 0], yr.at[h, k], S_YF + h, y_dev(k))

    def siblings(h, got, count, base):
        for j in range(count):
            width = 1 << j
            total = got[h, width]
            for k in range(width + 1, 2 * width):
                total = total + got[h, k]
            mean = (total * (1.0 / width)).astype(BF16)
            kc[h, pl.ds((base + j) * crows, crows), :] = mean[:crows]
            vc[h, pl.ds((base + j) * crows, crows), :] = mean[crows:]

    for h in range(2):
        drain(yr.at[h, pl.ds(1, ny - 1)], recv.at[S_YF + h])
        total = yr[h, 0]
        for k in range(1, ny):
            total = total + yr[h, k]
        zr[h, 0] = total * (1.0 / ny)
        for k in range(1, nz):
            remote(zr.at[h, 0], zr.at[h, k], S_ZF + h, z_dev(k))
        siblings(h, yr, ly, 0)
    for h in range(2):
        drain(zr.at[h, pl.ds(1, nz - 1)], recv.at[S_ZF + h])
        siblings(h, zr, lz, ly)

    drain(kr, recv.at[S_K])
    drain(vr, recv.at[S_V])

    row_level = lax.broadcasted_iota(jnp.int32, (levels * crows, 1), 0) // crows
    offsets = jnp.zeros((levels * crows, 1), F32)
    for j in range(levels):
        offsets = jnp.where(row_level == j, math.log(float(rows) * 2.0**j), offsets)

    nt = (((1,), (1,)), ((), ()))
    nn = (((1,), (0,)), ((), ()))
    tn = (((0,), (0,)), ((), ()))

    def dot(a, b, dims):
        return lax.dot_general(a, b, dims, preferred_element_type=F32)

    def compute(h):
        hc = pl.ds(h * HD, HD)
        block = min(shard, 256)
        kf, vf = kr[:, hc], vr[:, hc]
        kcv, vcv = kc[h], vc[h]
        for b in range(shard // block):
            br = pl.ds(b * block, block)
            q, g = qr[br, hc], gr[br, hc]
            sf = dot(kf, q, nt) * scale
            sc = dot(kcv, q, nt) * scale + offsets
            top = jnp.maximum(
                jnp.max(sf, axis=0, keepdims=True), jnp.max(sc, axis=0, keepdims=True)
            )
            pf, pc = jnp.exp(sf - top), jnp.exp(sc - top)
            norm = 1.0 / (
                jnp.sum(pf, axis=0, keepdims=True) + jnp.sum(pc, axis=0, keepdims=True)
            )
            pf, pc = pf * norm, pc * norm
            pfl, pcl = pf.astype(BF16), pc.astype(BF16)
            os[h, br, :] = (dot(pfl, vf, tn) + dot(pcl, vcv, tn)).astype(BF16)
            df, dc = dot(vf, g, nt), dot(vcv, g, nt)
            delta = jnp.sum(pf * df, axis=0, keepdims=True) + jnp.sum(
                pc * dc, axis=0, keepdims=True
            )
            dsf = (scale * pf * (df - delta)).astype(BF16)
            dsc = (scale * pc * (dc - delta)).astype(BF16)
            dqs[h, br, :] = (dot(dsf, kf, tn) + dot(dsc, kcv, tn)).astype(BF16)
            for acc, val in (
                (dka, dot(dsf, q, nn)),
                (dva, dot(pfl, g, nn)),
                (dkc, dot(dsc, q, nn)),
                (dvc, dot(pcl, g, nn)),
            ):
                if b == 0:
                    acc[h] = val
                else:
                    acc[h] += val

    def scatter_out(src, h, which):
        out = outs[which]
        start = pl.multiple_of((h_me * 2 + h) * HD, HD)
        there = out.at[:, pl.ds(start, HD)]
        for s in order:
            remote(src.at[h, pl.ds(s * rows, rows), :], there, S_OUT + which, (s_me, behind(s)))
        pltpu.make_async_copy(src.at[h, pl.ds(0, rows), :], there, recv.at[S_OUT + which]).start()

    for h in range(2):
        drain(qr.at[:, pl.ds(h * HD, HD)], recv.at[S_Q + h])
        drain(gr.at[:, pl.ds(h * HD, HD)], recv.at[S_G + h])
        compute(h)
        for j in range(lz):
            at = pl.ds((ly + j) * crows, crows)
            weight = 2.0 ** -(ly + j)
            zs[h, j, pl.ds(0, crows), :] = dkc[h, at, :] * weight
            zs[h, j, pl.ds(crows, crows), :] = dvc[h, at, :] * weight
        for k in range(1, nz):
            remote(zs.at[h, k.bit_length() - 1], zb.at[h, k], S_ZB + h, z_dev(k))
        scatter_out(os, h, 0)
        scatter_out(dqs, h, 1)

    for h in range(2):
        drain(zb.at[h, pl.ds(1, nz - 1)], recv.at[S_ZB + h])
        total = zb[h, 1]
        for k in range(2, nz):
            total = total + zb[h, k]
        yb[h, 0] = total
        for j in range(ly):
            at = pl.ds(j * crows, crows)
            weight = 2.0**-j
            ys[h, j, pl.ds(0, crows), :] = total[:crows] + dkc[h, at, :] * weight
            ys[h, j, pl.ds(crows, crows), :] = total[crows:] + dvc[h, at, :] * weight
        for k in range(1, ny):
            remote(ys.at[h, k.bit_length() - 1], yb.at[h, k], S_YB + h, y_dev(k))
    for h in range(2):
        drain(yb.at[h, pl.ds(1, ny - 1)], recv.at[S_YB + h])
        total = yb[h, 0]
        for k in range(1, ny):
            total = total + yb[h, k]
        total = total * (1.0 / rows)
        for which, (acc, dst, base) in enumerate(((dka, dks, 0), (dva, dvs, crows))):
            for s in range(nh):
                at = pl.ds(s * rows, rows)
                dst[h, at, :] = (acc[h, at, :] + total[base + s : base + s + 1]).astype(BF16)
            scatter_out(dst, h, 2 + which)

    for which, out in enumerate(outs):
        drain(out, recv.at[S_OUT + which])

    drain(pr.at[pl.ds(1, nh - 1)], send.at[S_POOL])
    part = pl.ds(0, shard - rows)
    drain(kr.at[part], send.at[S_K])
    drain(vr.at[part], send.at[S_V])
    for h in range(2):
        hc = pl.ds(h * HD, HD)
        drain(qr.at[part, hc], send.at[S_Q + h])
        drain(gr.at[part, hc], send.at[S_G + h])
        drain(yr.at[h, pl.ds(1, ny - 1)], send.at[S_YF + h])
        drain(zr.at[h, pl.ds(1, nz - 1)], send.at[S_ZF + h])
        drain(zb.at[h, pl.ds(1, nz - 1)], send.at[S_ZB + h])
        drain(yb.at[h, pl.ds(1, ny - 1)], send.at[S_YB + h])
    for which in range(4):
        drain(kr.at[part], send.at[S_OUT + which])


def solution(mesh):
    seq, head = mesh.shape["seq"], mesh.shape["head"]
    depth = seq.bit_length() - 1
    ny = 1 << (depth // 2)
    nz = seq // ny
    nx = head // 2

    def on_device(queries, keys_in, values_in, grad_out):
        rows, width = queries.shape
        shard = rows * head
        levels = depth
        here = jax.ShapeDtypeStruct((rows, width), BF16)
        anywhere = pl.BlockSpec(memory_space=pl.ANY)
        vm = pltpu.VMEM
        return pl.pallas_call(
            functools.partial(kernel, (nx, ny, nz)),
            out_shape=(here,) * 4,
            in_specs=[anywhere] * 4,
            out_specs=(anywhere,) * 4,
            scratch_shapes=[
                vm((rows, width), BF16),
                vm((rows, width), BF16),
                vm((head, 8, HD), F32),
                vm((head, 8, HD), F32),
                vm((shard, 2 * HD), BF16),
                vm((shard, 2 * HD), BF16),
                vm((shard, 2 * HD), BF16),
                vm((shard, 2 * HD), BF16),
                vm((2, ny, 2 * head, HD), F32),
                vm((2, nz, 2 * head, HD), F32),
                vm((2, levels * head, HD), BF16),
                vm((2, levels * head, HD), BF16),
                vm((2, depth - depth // 2, 2 * head, HD), F32),
                vm((2, nz, 2 * head, HD), F32),
                vm((2, depth // 2, 2 * head, HD), F32),
                vm((2, ny, 2 * head, HD), F32),
                vm((2, shard, HD), BF16),
                vm((2, shard, HD), BF16),
                vm((2, shard, HD), BF16),
                vm((2, shard, HD), BF16),
                vm((2, shard, HD), F32),
                vm((2, shard, HD), F32),
                vm((2, levels * head, HD), F32),
                vm((2, levels * head, HD), F32),
                pltpu.SemaphoreType.DMA((2,)),
                pltpu.SemaphoreType.DMA((N_SEMS,)),
                pltpu.SemaphoreType.DMA((N_SEMS,)),
            ],
            compiler_params=pltpu.CompilerParams(
                collective_id=0, has_side_effects=True, vmem_limit_bytes=40 * 1024 * 1024
            ),
        )(queries, keys_in, values_in, grad_out)

    placed = P(("seq", "head"), None)
    return jax.shard_map(
        on_device, mesh=mesh, in_specs=(placed,) * 4, out_specs=(placed,) * 4, check_vma=False
    )
```

time: 217 us -> 80.8 us (0.37)
  waiting for transfers between devices: 98.3 us -> 0 us
  starting transfers between devices: 92.7 us -> 0 us
  Pallas kernels: 0 us -> 73.3 us
  local copies, waits for them, and re-layouts: 16.1 us -> 6.6 us
  matrix products: 4.03 us -> 0 us
  other arithmetic: 3.07 us -> 0 us
    pallas_call x0 -> x1, Pallas kernels: none -> 73.3 us  [on_device(): pl.pallas_call(functools.partial(kernel, (nx, ny, nz)), out_shape=(here,)...]
    all_to_all x8 -> x0, waiting for transfers between devices: 71.7 us -> none  [the longest x1 10.6 us: on_device(): lax.all_to_all(queries, 'head', split_axis=1, concat_axis=0, tiled=True)]
    all_to_all x8 -> x0, starting transfers between devices: 48.9 us -> none  [the longest x1 17.5 us: on_device(): lax.all_to_all(values_in, 'head', split_axis=1, concat_axis=0, tiled=True)]
    ppermute x12 -> x0, starting transfers between devices: 43.8 us -> none  [swapped(): return lax.ppermute(block, axis, route)]
    ppermute x12 -> x0, waiting for transfers between devices: 26.5 us -> none  [swapped(): return lax.ppermute(block, axis, route)]
    all_to_all x12 -> x0, local copies, waits for them, and re-layouts: 12.2 us -> none  [the longest x1 1.72 us: on_device(): lax.all_to_all(values_in, 'head', split_axis=1, concat_axis=0, tiled=True)]
    unnamed x15 -> x12, local copies, waits for them, and re-layouts: 1.05 us -> 6.6 us
    convert_element_type x3 -> x0, other arithmetic: 2.45 us -> none  [the longest x1 2.36 us: on_device(): (scale_q * probs * (dprob - jnp.sum(probs * dprob, axis=-1, keepdims=True...]
  transfers between devices with their start and end apart: 20 -> 0, of which waited for: 17 -> 0; matrix products, arithmetic and copies ran while one was open for 4% -> 0% of each run, Pallas kernels for 0% -> 0%
where the time goes in v1:
time: 80.8 us; the launch traced here: 80.5 us
  Pallas kernels  73.3 us (91%)
  local copies, waits for them, and re-layouts  6.6 us (8%)
    pallas_call x1, Pallas kernels, on_device(): pl.pallas_call(functools.partial(kernel, (nx, ny, nz)), out_shape=(here,)...  73.3 us
    unnamed x12, local copies, waits for them, and re-layouts  6.6 us

profile of v1, /device:TPU:1, one launch (start us, length us, event | category | flops | bytes accessed | tf_op | source)
XLA Modules:
  0.0 80.5 jit_solution(17149953519853309305)
XLA Ops:
  0.6 0.0 copy-start
  0.6 0.9 %copy-done = bf16[32,4096]{1,0:T(8,128)(2,1)S(1)} copy-done((bf16[32,4096]{1,0:T(8,128)(2,1)S(1)}, bf16[32,4096]{1,0:T(8,128)(2,1)}, u32[]{:S(2)}) %copy-start) | copy-done | bytes 262168
  1.6 0.0 copy-start.1
  1.6 0.9 %copy-done.1 = bf16[32,4096]{1,0:T(8,128)(2,1)S(1)} copy-done((bf16[32,4096]{1,0:T(8,128)(2,1)S(1)}, bf16[32,4096]{1,0:T(8,128)(2,1)}, u32[]{:S(2)}) %copy-start.1) | copy-done | bytes 262168
  2.5 0.0 copy-start.2
  2.5 0.9 %copy-done.2 = bf16[32,4096]{1,0:T(8,128)(2,1)S(1)} copy-done((bf16[32,4096]{1,0:T(8,128)(2,1)S(1)}, bf16[32,4096]{1,0:T(8,128)(2,1)}, u32[]{:S(2)}) %copy-start.2) | copy-done | bytes 262168
  3.5 0.0 copy-start.3
  3.5 0.9 %copy-done.3 = bf16[32,4096]{1,0:T(8,128)(2,1)S(1)} copy-done((bf16[32,4096]{1,0:T(8,128)(2,1)S(1)}, bf16[32,4096]{1,0:T(8,128)(2,1)}, u32[]{:S(2)}) %copy-start.3) | copy-done | bytes 262168
  4.4 73.3 %shard_map.75 = (bf16[32,4096]{1,0:T(8,128)(2,1)S(1)}, bf16[32,4096]{1,0:T(8,128)(2,1)S(1)}, bf16[32,4096]{1,0:T(8,128)(2,1)S(1)}, bf16[32,4096]{1,0:T(8,128)(2,1)S(1)}) custom-call(bf16[32,4096]{1,0:T(8,128)(2,1)S(1)} %copy-done, bf16[32,4096]{1,0:T(8,128)(2,1)S(1)} %copy-done.1, bf16[32,4096]{1,0:T(8,128)(2,1)S(1)} %copy-done.2, bf16[32,4096]{1,0:T(8,128)(2,1)S(1)} %copy-done.3), custom_call_target="tpu_custom_call" | custom-call | tf_op jit(solution)/shard_map/pallas_call | solution.py:288
  77.7 0.7 copy.12
  78.4 0.7 copy.13
  79.1 0.7 copy.14
  79.8 0.7 copy.15
Async XLA Ops:
  0.6 1.0 %copy-start = (bf16[32,4096]{1,0:T(8,128)(2,1)S(1)}, bf16[32,4096]{1,0:T(8,128)(2,1)}, u32[]{:S(2)}) copy-start(bf16[32,4096]{1,0:T(8,128)(2,1)} %refs_0_.1) | copy-start | bytes 786436
  1.6 0.9 %copy-start.1 = (bf16[32,4096]{1,0:T(8,128)(2,1)S(1)}, bf16[32,4096]{1,0:T(8,128)(2,1)}, u32[]{:S(2)}) copy-start(bf16[32,4096]{1,0:T(8,128)(2,1)} %refs_1_.1) | copy-start | bytes 786436
  2.5 0.9 %copy-start.2 = (bf16[32,4096]{1,0:T(8,128)(2,1)S(1)}, bf16[32,4096]{1,0:T(8,128)(2,1)}, u32[]{:S(2)}) copy-start(bf16[32,4096]{1,0:T(8,128)(2,1)} %refs_2_.1) | copy-start | bytes 786436
  3.5 0.9 %copy-start.3 = (bf16[32,4096]{1,0:T(8,128)(2,1)S(1)}, bf16[32,4096]{1,0:T(8,128)(2,1)}, u32[]{:S(2)}) copy-start(bf16[32,4096]{1,0:T(8,128)(2,1)} %refs_3_.1) | copy-start | bytes 786436

commit v2 on v1

--- a/solution.py
+++ b/solution.py
@@ -13,8 +13,8 @@
 F32 = jnp.float32
 BF16 = jnp.bfloat16
 
-S_POOL, S_K, S_V, S_Q, S_G, S_YF, S_ZF, S_ZB, S_YB, S_OUT = 0, 1, 2, 3, 5, 7, 9, 11, 13, 15
-N_SEMS = 19
+S_POOL, S_K, S_V, S_Q, S_G, S_YF, S_ZF, S_ZB, S_YB, S_OUT, S_GX = 0, 1, 2, 3, 5, 7, 9, 11, 13, 15, 19
+N_SEMS = 20
 
 
 def flip(index, mask):
@@ -29,9 +29,9 @@
 
 def kernel(sizes, *refs):
     nx, ny, nz = sizes
-    (q_in, k_in, v_in, g_in, o_out, dq_out, dk_out, dv_out,
+    (q_in, k_in, v_in, g_in, o_out, dq_out, dk_out, dv_out, gx_out,
      kl, vl, ps, pr, qr, kr, vr, gr, yr, zr, kc, vc, zs, zb, ys, yb,
-     os, dqs, dks, dvs, dka, dva, dkc, dvc, local_sem, send, recv) = refs
+     gs, os, dqs, dks, dvs, dka, dva, dkc, dvc, local_sem, send, recv, go) = refs
     ins = (q_in, k_in, v_in, g_in)
     outs = (o_out, dq_out, dk_out, dv_out)
     nh = nx * 2
@@ -71,13 +71,10 @@
     vcopy = pltpu.make_async_copy(v_in, vl, local_sem.at[1])
     kcopy.start()
     vcopy.start()
+
     barrier = pltpu.get_barrier_semaphore()
     for s in order:
         pl.semaphore_signal(barrier, inc=1, device_id=(s_me, ahead(s)), device_id_type=MESH)
-    for k in range(1, ny):
-        pl.semaphore_signal(barrier, inc=1, device_id=y_dev(k), device_id_type=MESH)
-    for k in range(1, nz):
-        pl.semaphore_signal(barrier, inc=1, device_id=z_dev(k), device_id_type=MESH)
 
     kcopy.wait()
     vcopy.wait()
@@ -88,7 +85,18 @@
                 mean = jnp.sum(ref[:, cols].astype(F32), axis=0, keepdims=True) * (1.0 / rows)
                 ps[d, pl.ds(h * 2 + kv, 1), :] = mean
 
-    pl.semaphore_wait(barrier, len(order) + ny - 1 + nz - 1)
+    lines = [y_dev(k)[0] for k in range(1, ny)] + [z_dev(k)[0] for k in range(1, nz)]
+    pl.semaphore_wait(barrier, len(order) + jnp.where(h_me == 0, len(lines), 0))
+
+    @pl.when(h_me == 1)
+    def _():
+        for line in lines:
+            pl.semaphore_signal(barrier, inc=1, device_id=(line, 0), device_id_type=MESH)
+
+    @pl.when(h_me == 0)
+    def _():
+        for d in range(1, nh):
+            pl.semaphore_signal(go, inc=1, device_id=(s_me, d), device_id_type=MESH)
 
     def remote(src, dst, sem, device):
         pltpu.make_async_remote_copy(
@@ -98,11 +106,6 @@
 
     def drain(ref, sem):
         pltpu.make_async_copy(ref, ref, sem).wait()
-
-    for s in order:
-        d = ahead(s)
-        remote(ps.at[d], pr.at[s], S_POOL, (s_me, d))
-    pr[0] = ps[h_me]
 
     def scatter_in(src, dst, sem, first, width):
         def piece(d):
@@ -116,6 +119,11 @@
             piece(h_me), dst.at[pl.ds(0, rows), pl.ds(first, width)], recv.at[sem]
         ).start()
 
+    for s in order:
+        d = ahead(s)
+        remote(ps.at[d], pr.at[s], S_POOL, (s_me, d))
+    pr[0] = ps[h_me]
+
     scatter_in(k_in, kr, S_K, 0, 2 * HD)
     scatter_in(v_in, vr, S_V, 0, 2 * HD)
     for h in range(2):
@@ -123,6 +131,11 @@
         scatter_in(g_in, gr, S_G + h, h * HD, HD)
 
     drain(pr.at[pl.ds(1, nh - 1)], recv.at[S_POOL])
+
+    @pl.when(h_me != 0)
+    def _():
+        pl.semaphore_wait(go, 1)
+
     for h in range(2):
         for kv in range(2):
             yr[h, 0, pl.ds(kv * crows, crows), :] = pr[:, h * 2 + kv, :]
@@ -148,13 +161,6 @@
         for k in range(1, nz):
             remote(zr.at[h, 0], zr.at[h, k], S_ZF + h, z_dev(k))
         siblings(h, yr, ly, 0)
-    for h in range(2):
-        drain(zr.at[h, pl.ds(1, nz - 1)], recv.at[S_ZF + h])
-        siblings(h, zr, lz, ly)
-
-    drain(kr, recv.at[S_K])
-    drain(vr, recv.at[S_V])
-
     row_level = lax.broadcasted_iota(jnp.int32, (levels * crows, 1), 0) // crows
     offsets = jnp.zeros((levels * crows, 1), F32)
     for j in range(levels):
@@ -167,12 +173,14 @@
     def dot(a, b, dims):
         return lax.dot_general(a, b, dims, preferred_element_type=F32)
 
-    def compute(h):
+    def compute(h, between):
         hc = pl.ds(h * HD, HD)
         block = min(shard, 256)
         kf, vf = kr[:, hc], vr[:, hc]
         kcv, vcv = kc[h], vc[h]
         for b in range(shard // block):
+            if b == shard // block - 1 and between is not None:
+                between()
             br = pl.ds(b * block, block)
             q, g = qr[br, hc], gr[br, hc]
             sf = dot(kf, q, nt) * scale
@@ -213,21 +221,7 @@
             remote(src.at[h, pl.ds(s * rows, rows), :], there, S_OUT + which, (s_me, behind(s)))
         pltpu.make_async_copy(src.at[h, pl.ds(0, rows), :], there, recv.at[S_OUT + which]).start()
 
-    for h in range(2):
-        drain(qr.at[:, pl.ds(h * HD, HD)], recv.at[S_Q + h])
-        drain(gr.at[:, pl.ds(h * HD, HD)], recv.at[S_G + h])
-        compute(h)
-        for j in range(lz):
-            at = pl.ds((ly + j) * crows, crows)
-            weight = 2.0 ** -(ly + j)
-            zs[h, j, pl.ds(0, crows), :] = dkc[h, at, :] * weight
-            zs[h, j, pl.ds(crows, crows), :] = dvc[h, at, :] * weight
-        for k in range(1, nz):
-            remote(zs.at[h, k.bit_length() - 1], zb.at[h, k], S_ZB + h, z_dev(k))
-        scatter_out(os, h, 0)
-        scatter_out(dqs, h, 1)
-
-    for h in range(2):
+    def back_along_y(h):
         drain(zb.at[h, pl.ds(1, nz - 1)], recv.at[S_ZB + h])
         total = zb[h, 1]
         for k in range(2, nz):
@@ -240,20 +234,43 @@
             ys[h, j, pl.ds(crows, crows), :] = total[crows:] + dvc[h, at, :] * weight
         for k in range(1, ny):
             remote(ys.at[h, k.bit_length() - 1], yb.at[h, k], S_YB + h, y_dev(k))
+
+    drain(kr, recv.at[S_K])
+    drain(vr, recv.at[S_V])
+    for h in range(2):
+        drain(zr.at[h, pl.ds(1, nz - 1)], recv.at[S_ZF + h])
+        siblings(h, zr, lz, ly)
+        drain(qr.at[:, pl.ds(h * HD, HD)], recv.at[S_Q + h])
+        drain(gr.at[:, pl.ds(h * HD, HD)], recv.at[S_G + h])
+        compute(h, (lambda: back_along_y(0)) if h else None)
+        for j in range(lz):
+            at = pl.ds((ly + j) * crows, crows)
+            weight = 2.0 ** -(ly + j)
+            zs[h, j, pl.ds(0, crows), :] = dkc[h, at, :] * weight
+            zs[h, j, pl.ds(crows, crows), :] = dvc[h, at, :] * weight
+        for k in range(1, nz):
+            remote(zs.at[h, k.bit_length() - 1], zb.at[h, k], S_ZB + h, z_dev(k))
+        dks[h] = dka[h].astype(BF16)
+        dvs[h] = dva[h].astype(BF16)
+        for which, staged in enumerate((os, dqs, dks, dvs)):
+            scatter_out(staged, h, which)
+
+    back_along_y(1)
     for h in range(2):
         drain(yb.at[h, pl.ds(1, ny - 1)], recv.at[S_YB + h])
         total = yb[h, 0]
         for k in range(1, ny):
             total = total + yb[h, k]
         total = total * (1.0 / rows)
-        for which, (acc, dst, base) in enumerate(((dka, dks, 0), (dva, dvs, crows))):
-            for s in range(nh):
-                at = pl.ds(s * rows, rows)
-                dst[h, at, :] = (acc[h, at, :] + total[base + s : base + s + 1]).astype(BF16)
-            scatter_out(dst, h, 2 + which)
+        gs[:, h * 2, :] = total[:crows]
+        gs[:, h * 2 + 1, :] = total[crows:]
+    for s in order:
+        remote(gs.at[s], gx_out.at[h_me], S_GX, (s_me, behind(s)))
+    pltpu.make_async_copy(gs.at[0], gx_out.at[h_me], recv.at[S_GX]).start()
 
     for which, out in enumerate(outs):
         drain(out, recv.at[S_OUT + which])
+    drain(gx_out, recv.at[S_GX])
 
     drain(pr.at[pl.ds(1, nh - 1)], send.at[S_POOL])
     part = pl.ds(0, shard - rows)
@@ -269,6 +286,31 @@
         drain(yb.at[h, pl.ds(1, ny - 1)], send.at[S_YB + h])
     for which in range(4):
         drain(kr.at[part], send.at[S_OUT + which])
+    drain(gs.at[pl.ds(1, nh - 1)], send.at[S_GX])
+
+
+def put_out(*refs):
+    arrived, placed = refs[:5], refs[5:9]
+    staged, pooled, sems = refs[9:]
+    ins = [staged.at[i] for i in range(4)] + [pooled]
+    first = [pltpu.make_async_copy(arrived[i], ins[i], sems.at[0, i]) for i in range(5)]
+    last = [pltpu.make_async_copy(staged.at[i], placed[i], sems.at[1, i]) for i in range(4)]
+    for copy in first:
+        copy.start()
+    for i in range(2):
+        first[i].wait()
+        last[i].start()
+    first[4].wait()
+    for kv in range(2):
+        first[2 + kv].wait()
+        for d in range(pooled.shape[0]):
+            for h in range(2):
+                cols = pl.ds((d * 2 + h) * HD, HD)
+                row = pooled[d, pl.ds(h * 2 + kv, 1), :]
+                staged[2 + kv, :, cols] = (staged[2 + kv, :, cols].astype(F32) + row).astype(BF16)
+        last[2 + kv].start()
+    for copy in last:
+        copy.wait()
 
 
 def solution(mesh):
@@ -285,16 +327,16 @@
         here = jax.ShapeDtypeStruct((rows, width), BF16)
         anywhere = pl.BlockSpec(memory_space=pl.ANY)
         vm = pltpu.VMEM
-        return pl.pallas_call(
+        results = pl.pallas_call(
             functools.partial(kernel, (nx, ny, nz)),
-            out_shape=(here,) * 4,
+            out_shape=(here,) * 4 + (jax.ShapeDtypeStruct((head, 4, HD), F32),),
             in_specs=[anywhere] * 4,
-            out_specs=(anywhere,) * 4,
+            out_specs=(anywhere,) * 5,
             scratch_shapes=[
                 vm((rows, width), BF16),
                 vm((rows, width), BF16),
-                vm((head, 8, HD), F32),
-                vm((head, 8, HD), F32),
+                vm((head, 4, HD), F32),
+                vm((head, 4, HD), F32),
                 vm((shard, 2 * HD), BF16),
                 vm((shard, 2 * HD), BF16),
                 vm((shard, 2 * HD), BF16),
@@ -307,6 +349,7 @@
                 vm((2, nz, 2 * head, HD), F32),
                 vm((2, depth // 2, 2 * head, HD), F32),
                 vm((2, ny, 2 * head, HD), F32),
+                vm((head, 4, HD), F32),
                 vm((2, shard, HD), BF16),
                 vm((2, shard, HD), BF16),
                 vm((2, shard, HD), BF16),
@@ -318,11 +361,24 @@
                 pltpu.SemaphoreType.DMA((2,)),
                 pltpu.SemaphoreType.DMA((N_SEMS,)),
                 pltpu.SemaphoreType.DMA((N_SEMS,)),
+                pltpu.SemaphoreType.REGULAR,
             ],
             compiler_params=pltpu.CompilerParams(
-                collective_id=0, has_side_effects=True, vmem_limit_bytes=40 * 1024 * 1024
+                collective_id=0, has_side_effects=True, vmem_limit_bytes=67043328
             ),
         )(queries, keys_in, values_in, grad_out)
+        return pl.pallas_call(
+            put_out,
+            out_shape=(here,) * 4,
+            in_specs=[anywhere] * 5,
+            out_specs=(anywhere,) * 4,
+            scratch_shapes=[
+                vm((4, rows, width), BF16),
+                vm((head, 4, HD), F32),
+                pltpu.SemaphoreType.DMA((2, 5)),
+            ],
+            compiler_params=pltpu.CompilerParams(vmem_limit_bytes=67043328),
+        )(*results)
 
     placed = P(("seq", "head"), None)
     return jax.shard_map(

time: 80.8 us -> 74.7 us (0.925)
  local copies, waits for them, and re-layouts: 6.6 us -> 0 us
    unnamed x12 -> x0, local copies, waits for them, and re-layouts: 6.6 us -> none
    pallas_call x0 -> x1, Pallas kernels: none -> 2.04 us  [on_device(): pl.pallas_call(put_out, out_shape=(here,) * 4, in_specs=[anywhere] * 5, o...]
    pallas_call x1, Pallas kernels: 73.3 us -> 71.8 us  [on_device(): pl.pallas_call(functools.partial(kernel, (nx, ny, nz)), out_shape=(here,)...]
where the time goes in v2:
time: 74.7 us; the launch traced here: 74.5 us
  Pallas kernels  73.9 us (99%)
    pallas_call x1, Pallas kernels, on_device(): pl.pallas_call(functools.partial(kernel, (nx, ny, nz)), out_shape=(here,)...  71.8 us
    pallas_call x1, Pallas kernels, on_device(): pl.pallas_call(put_out, out_shape=(here,) * 4, in_specs=[anywhere] * 5, o...  2.04 us

profile of v2, /device:TPU:1, one launch (start us, length us, event | category | flops | bytes accessed | tf_op | source)
XLA Modules:
  0.0 74.5 jit_solution(11109095559160325313)
XLA Ops:
  0.6 71.8 %shard_map.75 = (bf16[32,4096]{1,0:T(8,128)(2,1)}, bf16[32,4096]{1,0:T(8,128)(2,1)}, bf16[32,4096]{1,0:T(8,128)(2,1)}, bf16[32,4096]{1,0:T(8,128)(2,1)}, f32[16,4,128]{2,1,0:T(4,128)}) custom-call(bf16[32,4096]{1,0:T(8,128)(2,1)} %refs_0_.1, bf16[32,4096]{1,0:T(8,128)(2,1)} %refs_1_.1, bf16[32,4096]{1,0:T(8,128)(2,1)} %refs_2_.1, bf16[32,4096]{1,0:T(8,128)(2,1)} %refs_3_.1), custom_call_target="tpu_custom_call" | custom-call | tf_op jit(solution)/shard_map/pallas_call | solution.py:330
  72.5 2.0 %shard_map.76 = (bf16[32,4096]{1,0:T(8,128)(2,1)}, bf16[32,4096]{1,0:T(8,128)(2,1)}, bf16[32,4096]{1,0:T(8,128)(2,1)}, bf16[32,4096]{1,0:T(8,128)(2,1)}) custom-call(bf16[32,4096]{1,0:T(8,128)(2,1)} %get-tuple-element.9.refs_0_, bf16[32,4096]{1,0:T(8,128)(2,1)} %get-tuple-element.10.refs_1_, bf16[32,4096]{1,0:T(8,128)(2,1)} %get-tuple-element.11.refs_2_, ...), custom_call_target="tpu_custom_call" | custom-call | tf_op jit(solution)/shard_map/pallas_call | solution.py:370

commit v3 on v2

--- a/solution.py
+++ b/solution.py
@@ -31,7 +31,7 @@
     nx, ny, nz = sizes
     (q_in, k_in, v_in, g_in, o_out, dq_out, dk_out, dv_out, gx_out,
      kl, vl, ps, pr, qr, kr, vr, gr, yr, zr, kc, vc, zs, zb, ys, yb,
-     gs, os, dqs, dks, dvs, dka, dva, dkc, dvc, local_sem, send, recv, go) = refs
+     za, pk, dsk, gs, os, dqs, dks, dvs, dkc, dvc, local_sem, send, recv, go) = refs
     ins = (q_in, k_in, v_in, g_in)
     outs = (o_out, dq_out, dk_out, dv_out)
     nh = nx * 2
@@ -61,6 +61,9 @@
             order += [2 * kk, 2 * kk + 1]
     order = [s for s in order if s != 0]
 
+    def far_first(count):
+        return sorted(range(1, count), key=lambda k: (-min(k, count - k), k))
+
     def y_dev(k):
         return (z_me * ny + flip(y_me, k), h_me)
 
@@ -139,7 +142,7 @@
     for h in range(2):
         for kv in range(2):
             yr[h, 0, pl.ds(kv * crows, crows), :] = pr[:, h * 2 + kv, :]
-        for k in range(1, ny):
+        for k in far_first(ny):
             remote(yr.at[h, 0], yr.at[h, k], S_YF + h, y_dev(k))
 
     def siblings(h, got, count, base):
@@ -158,7 +161,7 @@
         for k in range(1, ny):
             total = total + yr[h, k]
         zr[h, 0] = total * (1.0 / ny)
-        for k in range(1, nz):
+        for k in far_first(nz):
             remote(zr.at[h, 0], zr.at[h, k], S_ZF + h, z_dev(k))
         siblings(h, yr, ly, 0)
     row_level = lax.broadcasted_iota(jnp.int32, (levels * crows, 1), 0) // crows
@@ -173,7 +176,9 @@
     def dot(a, b, dims):
         return lax.dot_general(a, b, dims, preferred_element_type=F32)
 
-    def compute(h, between):
+    fine, coarse = pl.ds(0, shard), pl.ds(shard, levels * crows)
+
+    def scores(h, between):
         hc = pl.ds(h * HD, HD)
         block = min(shard, 256)
         kf, vf = kr[:, hc], vr[:, hc]
@@ -193,25 +198,24 @@
                 jnp.sum(pf, axis=0, keepdims=True) + jnp.sum(pc, axis=0, keepdims=True)
             )
             pf, pc = pf * norm, pc * norm
-            pfl, pcl = pf.astype(BF16), pc.astype(BF16)
-            os[h, br, :] = (dot(pfl, vf, tn) + dot(pcl, vcv, tn)).astype(BF16)
+            pk[fine, br] = pf.astype(BF16)
+            pk[coarse, br] = pc.astype(BF16)
             df, dc = dot(vf, g, nt), dot(vcv, g, nt)
             delta = jnp.sum(pf * df, axis=0, keepdims=True) + jnp.sum(
                 pc * dc, axis=0, keepdims=True
             )
-            dsf = (scale * pf * (df - delta)).astype(BF16)
-            dsc = (scale * pc * (dc - delta)).astype(BF16)
-            dqs[h, br, :] = (dot(dsf, kf, tn) + dot(dsc, kcv, tn)).astype(BF16)
-            for acc, val in (
-                (dka, dot(dsf, q, nn)),
-                (dva, dot(pfl, g, nn)),
-                (dkc, dot(dsc, q, nn)),
-                (dvc, dot(pcl, g, nn)),
-            ):
-                if b == 0:
-                    acc[h] = val
-                else:
-                    acc[h] += val
+            dsk[fine, br] = (scale * pf * (df - delta)).astype(BF16)
+            dsk[coarse, br] = (scale * pc * (dc - delta)).astype(BF16)
+        dkc[h] = dot(dsk[coarse, :], qr[:, hc], nn)
+        dvc[h] = dot(pk[coarse, :], gr[:, hc], nn)
+
+    def products(h):
+        hc = pl.ds(h * HD, HD)
+        kf, vf, kcv, vcv = kr[:, hc], vr[:, hc], kc[h], vc[h]
+        os[h] = (dot(pk[fine, :], vf, tn) + dot(pk[coarse, :], vcv, tn)).astype(BF16)
+        dqs[h] = (dot(dsk[fine, :], kf, tn) + dot(dsk[coarse, :], kcv, tn)).astype(BF16)
+        dks[h] = dot(dsk[fine, :], qr[:, hc], nn).astype(BF16)
+        dvs[h] = dot(pk[fine, :], gr[:, hc], nn).astype(BF16)
 
     def scatter_out(src, h, which):
         out = outs[which]
@@ -223,16 +227,18 @@
 
     def back_along_y(h):
         drain(zb.at[h, pl.ds(1, nz - 1)], recv.at[S_ZB + h])
-        total = zb[h, 1]
+        total = zb[h, 1].astype(F32)
         for k in range(2, nz):
-            total = total + zb[h, k]
-        yb[h, 0] = total
+            total = total + zb[h, k].astype(F32)
+        za[h] = total
         for j in range(ly):
             at = pl.ds(j * crows, crows)
             weight = 2.0**-j
-            ys[h, j, pl.ds(0, crows), :] = total[:crows] + dkc[h, at, :] * weight
-            ys[h, j, pl.ds(crows, crows), :] = total[crows:] + dvc[h, at, :] * weight
-        for k in range(1, ny):
+            key_part = total[:crows] + dkc[h, at, :] * weight
+            value_part = total[crows:] + dvc[h, at, :] * weight
+            ys[h, j, pl.ds(0, crows), :] = key_part.astype(BF16)
+            ys[h, j, pl.ds(crows, crows), :] = value_part.astype(BF16)
+        for k in far_first(ny):
             remote(ys.at[h, k.bit_length() - 1], yb.at[h, k], S_YB + h, y_dev(k))
 
     drain(kr, recv.at[S_K])
@@ -242,31 +248,33 @@
         siblings(h, zr, lz, ly)
         drain(qr.at[:, pl.ds(h * HD, HD)], recv.at[S_Q + h])
         drain(gr.at[:, pl.ds(h * HD, HD)], recv.at[S_G + h])
-        compute(h, (lambda: back_along_y(0)) if h else None)
+        scores(h, (lambda: back_along_y(0)) if h else None)
         for j in range(lz):
             at = pl.ds((ly + j) * crows, crows)
             weight = 2.0 ** -(ly + j)
-            zs[h, j, pl.ds(0, crows), :] = dkc[h, at, :] * weight
-            zs[h, j, pl.ds(crows, crows), :] = dvc[h, at, :] * weight
-        for k in range(1, nz):
+            zs[h, j, pl.ds(0, crows), :] = (dkc[h, at, :] * weight).astype(BF16)
+            zs[h, j, pl.ds(crows, crows), :] = (dvc[h, at, :] * weight).astype(BF16)
+        for k in far_first(nz):
             remote(zs.at[h, k.bit_length() - 1], zb.at[h, k], S_ZB + h, z_dev(k))
-        dks[h] = dka[h].astype(BF16)
-        dvs[h] = dva[h].astype(BF16)
+        products(h)
+        if h == 1:
+            back_along_y(1)
         for which, staged in enumerate((os, dqs, dks, dvs)):
-            scatter_out(staged, h, which)
-
-    back_along_y(1)
+            if (h, which) != (1, 3):
+                scatter_out(staged, h, which)
+
     for h in range(2):
         drain(yb.at[h, pl.ds(1, ny - 1)], recv.at[S_YB + h])
-        total = yb[h, 0]
+        total = za[h]
         for k in range(1, ny):
-            total = total + yb[h, k]
+            total = total + yb[h, k].astype(F32)
         total = total * (1.0 / rows)
         gs[:, h * 2, :] = total[:crows]
         gs[:, h * 2 + 1, :] = total[crows:]
     for s in order:
         remote(gs.at[s], gx_out.at[h_me], S_GX, (s_me, behind(s)))
     pltpu.make_async_copy(gs.at[0], gx_out.at[h_me], recv.at[S_GX]).start()
+    scatter_out(dvs, 1, 3)
 
     for which, out in enumerate(outs):
         drain(out, recv.at[S_OUT + which])
@@ -345,17 +353,18 @@
                 vm((2, nz, 2 * head, HD), F32),
                 vm((2, levels * head, HD), BF16),
                 vm((2, levels * head, HD), BF16),
-                vm((2, depth - depth // 2, 2 * head, HD), F32),
-                vm((2, nz, 2 * head, HD), F32),
-                vm((2, depth // 2, 2 * head, HD), F32),
-                vm((2, ny, 2 * head, HD), F32),
+                vm((2, depth - depth // 2, 2 * head, HD), BF16),
+                vm((2, nz, 2 * head, HD), BF16),
+                vm((2, depth // 2, 2 * head, HD), BF16),
+                vm((2, ny, 2 * head, HD), BF16),
+                vm((2, 2 * head, HD), F32),
+                vm((shard + levels * head, shard), BF16),
+                vm((shard + levels * head, shard), BF16),
                 vm((head, 4, HD), F32),
                 vm((2, shard, HD), BF16),
                 vm((2, shard, HD), BF16),
                 vm((2, shard, HD), BF16),
                 vm((2, shard, HD), BF16),
-                vm((2, shard, HD), F32),
-                vm((2, shard, HD), F32),
                 vm((2, levels * head, HD), F32),
                 vm((2, levels * head, HD), F32),
                 pltpu.SemaphoreType.DMA((2,)),

time: 74.7 us -> 71.4 us (0.956)
  Pallas kernels: 73.9 us -> 70.6 us
    pallas_call x1, Pallas kernels: 71.8 us -> 68.5 us  [on_device(): pl.pallas_call(functools.partial(kernel, (nx, ny, nz)), out_shape=(here,)...]
where the time goes in v3:
time: 71.4 us; the launch traced here: 71.2 us
  Pallas kernels  70.6 us (99%)
    pallas_call x1, Pallas kernels, on_device(): pl.pallas_call(functools.partial(kernel, (nx, ny, nz)), out_shape=(here,)...  68.5 us
    pallas_call x1, Pallas kernels, on_device(): pl.pallas_call(put_out, out_shape=(here,) * 4, in_specs=[anywhere] * 5, o...  2.04 us

profile of v3, /device:TPU:1, one launch (start us, length us, event | category | flops | bytes accessed | tf_op | source)
XLA Modules:
  0.0 71.2 jit_solution(13274525136161333249)
XLA Ops:
  0.6 68.5 %shard_map.75 = (bf16[32,4096]{1,0:T(8,128)(2,1)}, bf16[32,4096]{1,0:T(8,128)(2,1)}, bf16[32,4096]{1,0:T(8,128)(2,1)}, bf16[32,4096]{1,0:T(8,128)(2,1)}, f32[16,4,128]{2,1,0:T(4,128)}) custom-call(bf16[32,4096]{1,0:T(8,128)(2,1)} %refs_0_.1, bf16[32,4096]{1,0:T(8,128)(2,1)} %refs_1_.1, bf16[32,4096]{1,0:T(8,128)(2,1)} %refs_2_.1, bf16[32,4096]{1,0:T(8,128)(2,1)} %refs_3_.1), custom_call_target="tpu_custom_call" | custom-call | tf_op jit(solution)/shard_map/pallas_call | solution.py:338
  69.2 2.0 %shard_map.76 = (bf16[32,4096]{1,0:T(8,128)(2,1)}, bf16[32,4096]{1,0:T(8,128)(2,1)}, bf16[32,4096]{1,0:T(8,128)(2,1)}, bf16[32,4096]{1,0:T(8,128)(2,1)}) custom-call(bf16[32,4096]{1,0:T(8,128)(2,1)} %get-tuple-element.9.refs_0_, bf16[32,4096]{1,0:T(8,128)(2,1)} %get-tuple-element.10.refs_1_, bf16[32,4096]{1,0:T(8,128)(2,1)} %get-tuple-element.11.refs_2_, ...), custom_call_target="tpu_custom_call" | custom-call | tf_op jit(solution)/shard_map/pallas_call | solution.py:379

commit v4 on v3

--- a/solution.py
+++ b/solution.py
@@ -248,7 +248,7 @@
         siblings(h, zr, lz, ly)
         drain(qr.at[:, pl.ds(h * HD, HD)], recv.at[S_Q + h])
         drain(gr.at[:, pl.ds(h * HD, HD)], recv.at[S_G + h])
-        scores(h, (lambda: back_along_y(0)) if h else None)
+        scores(h, None)
         for j in range(lz):
             at = pl.ds((ly + j) * crows, crows)
             weight = 2.0 ** -(ly + j)
@@ -256,6 +256,8 @@
             zs[h, j, pl.ds(crows, crows), :] = (dvc[h, at, :] * weight).astype(BF16)
         for k in far_first(nz):
             remote(zs.at[h, k.bit_length() - 1], zb.at[h, k], S_ZB + h, z_dev(k))
+        if h == 1:
+            back_along_y(0)
         products(h)
         if h == 1:
             back_along_y(1)

time: 71.4 us -> 71.4 us (level)
  no operation moved by 1% of the time
where the time goes in v4:
time: 71.4 us; the launch traced here: 71.2 us
  Pallas kernels  70.6 us (99%)
    pallas_call x1, Pallas kernels, on_device(): pl.pallas_call(functools.partial(kernel, (nx, ny, nz)), out_shape=(here,)...  68.6 us
    pallas_call x1, Pallas kernels, on_device(): pl.pallas_call(put_out, out_shape=(here,) * 4, in_specs=[anywhere] * 5, o...  2.04 us

profile of v4, /device:TPU:1, one launch (start us, length us, event | category | flops | bytes accessed | tf_op | source)
XLA Modules:
  0.0 71.2 jit_solution(5829991978039329200)
XLA Ops:
  0.6 68.6 %shard_map.75 = (bf16[32,4096]{1,0:T(8,128)(2,1)}, bf16[32,4096]{1,0:T(8,128)(2,1)}, bf16[32,4096]{1,0:T(8,128)(2,1)}, bf16[32,4096]{1,0:T(8,128)(2,1)}, f32[16,4,128]{2,1,0:T(4,128)}) custom-call(bf16[32,4096]{1,0:T(8,128)(2,1)} %refs_0_.1, bf16[32,4096]{1,0:T(8,128)(2,1)} %refs_1_.1, bf16[32,4096]{1,0:T(8,128)(2,1)} %refs_2_.1, bf16[32,4096]{1,0:T(8,128)(2,1)} %refs_3_.1), custom_call_target="tpu_custom_call" | custom-call | tf_op jit(solution)/shard_map/pallas_call | solution.py:340
  69.2 2.0 %shard_map.76 = (bf16[32,4096]{1,0:T(8,128)(2,1)}, bf16[32,4096]{1,0:T(8,128)(2,1)}, bf16[32,4096]{1,0:T(8,128)(2,1)}, bf16[32,4096]{1,0:T(8,128)(2,1)}) custom-call(bf16[32,4096]{1,0:T(8,128)(2,1)} %get-tuple-element.9.refs_0_, bf16[32,4096]{1,0:T(8,128)(2,1)} %get-tuple-element.10.refs_1_, bf16[32,4096]{1,0:T(8,128)(2,1)} %get-tuple-element.11.refs_2_, ...), custom_call_target="tpu_custom_call" | custom-call | tf_op jit(solution)/shard_map/pallas_call | solution.py:381
